TPU v7x, 32 devices: a whole 2x2x4 slice. The times are simulated.
32 devices in a mesh: ctx: 8 (over z, x), tp: 4 (over y, core).
Axes of the slice: x: 2, y: 2, z: 4, core: 2. Of those that a mesh axis runs over, the one named last changes fastest.
Arguments:
- hidden: bfloat16 [1024, 3584], P('ctx', 'tp'), may hold values from -6 to 6
- norm_gain: float32 [3584], replicated, may hold values from 0.1 to 1.9
- w_query: bfloat16 [3584, 3584], P(None, 'tp'), may hold values from -0.09375 to 0.09375
- bias_query: float32 [3584], P('tp'), may hold values from -3 to 3
- w_key: bfloat16 [3584, 512], P(None, 'tp'), may hold values from -0.09375 to 0.09375
- bias_key: float32 [512], P('tp'), may hold values from -3 to 3
- w_value: bfloat16 [3584, 512], P(None, 'tp'), may hold values from -0.09375 to 0.09375
- bias_value: float32 [512], P('tp'), may hold values from -3 to 3
- cache_key: bfloat16 [2048, 512], P('ctx', 'tp'), may hold values from -64 to 64
- cache_value: bfloat16 [2048, 512], P('ctx', 'tp'), may hold values from -6 to 6
- keep: int32 [1024], replicated, may hold values from 0 to 1, as said below
- positions: int32 [3, 1024], replicated, may hold values from 0 to 2047
Outputs:
- attended: bfloat16 [1024, 3584], P('ctx', 'tp')
Inputs may be any that keep to these rules, and one draw needn't show every extreme that they name: `keep`: exactly 512 tokens are kept; the counts kept by the 128-token blocks differ widely, and some block keeps all of its tokens.
All inputs are finite; a program needn't handle non-finite values.
Results may differ from a plain program's by a relative error of at most 0.0075.
The roundings to bfloat16 on the way count: a program that leaves them out, or rounds other values in their place, can miss the bound.
Values may be sent and summed in bfloat16 or wider, within the bound.
No kernel may reach another device: no remote copies, remote signals or barrier semaphores. Data moves between devices by JAX's collectives and lax.ppermute only.
A program may use at most 128 MiB of HBM per device.

v0:
```python
import jax
import jax.numpy as jnp
from jax import lax
from jax.sharding import PartitionSpec as P

HD = 128


def rotate(flat, where):
    count = flat.shape[0]
    heads = flat.shape[1] // HD
    x = flat.reshape(count, heads, HD)
    half = HD // 2
    freq = jnp.arange(half)
    inv = jnp.exp(-(2.0 * freq.astype(jnp.float32) / HD) * jnp.log(jnp.float32(1000000.0)))
    section = jnp.where(freq < HD // 8, 0, jnp.where(freq < HD // 8 + 3 * HD // 16, 1, 2))
    picked = where[section, :].astype(jnp.float32).T
    angle = picked * inv[None, :]
    cosine = jnp.concatenate([jnp.cos(angle), jnp.cos(angle)], axis=1)[:, None, :]
    sine = jnp.concatenate([jnp.sin(angle), jnp.sin(angle)], axis=1)[:, None, :]
    turned = jnp.concatenate([-x[:, :, half:], x[:, :, :half]], axis=2)
    return (x * cosine + turned * sine).reshape(count, heads * HD)


def local(
    hidden,
    norm_gain,
    w_query,
    bias_query,
    w_key,
    bias_key,
    w_value,
    bias_value,
    cache_key,
    cache_value,
    keep,
    positions,
):
    n_ctx = lax.axis_size("ctx")
    rank = lax.axis_index("ctx")
    tok_rows = hidden.shape[0]
    cache_rows = cache_key.shape[0]
    kv_local = w_key.shape[1] // HD
    groups = w_query.shape[1] // w_key.shape[1]
    keep_blocks = keep.reshape(n_ctx, tok_rows)
    counts = jnp.sum(keep_blocks, axis=1)
    first = jnp.cumsum(counts) - counts
    ordinal_blocks = jnp.cumsum(keep_blocks, axis=1) - keep_blocks + first[:, None]
    own_start = rank * tok_rows
    own_keep = lax.dynamic_index_in_dim(keep_blocks, rank, 0, keepdims=False)
    own_order = lax.dynamic_index_in_dim(ordinal_blocks, rank, 0, keepdims=False)
    sentinel = 2**30
    query_live = own_keep.astype(jnp.float32)
    where = lax.dynamic_slice_in_dim(positions, own_start, tok_rows, 1)
    fresh_tag = jnp.where(keep_blocks > 0, ordinal_blocks, sentinel)
    count_rows = hidden.shape[0]
    key_tag = jnp.concatenate(
        [jnp.full((n_ctx, cache_rows), -1, jnp.int32), fresh_tag], axis=1
    ).reshape(-1)
    whole = lax.all_gather(hidden, "tp", axis=1, tiled=True)
    widened = whole.astype(jnp.float32)
    scale_row = lax.rsqrt(jnp.mean(widened * widened, axis=1, keepdims=True) + 1e-06)
    normed = (widened * scale_row * norm_gain[None, :]).astype(jnp.bfloat16)
    query = rotate(
        jnp.dot(normed, w_query, preferred_element_type=jnp.float32) + bias_query, where
    ).astype(jnp.bfloat16)
    query = query.reshape(count_rows, kv_local, groups, HD)
    fresh_key = rotate(
        jnp.dot(normed, w_key, preferred_element_type=jnp.float32) + bias_key, where
    ).astype(jnp.bfloat16)
    fresh_value = (
        jnp.dot(normed, w_value, preferred_element_type=jnp.float32) + bias_value
    ).astype(jnp.bfloat16)
    keys = jnp.concatenate([cache_key, fresh_key], axis=0)
    values = jnp.concatenate([cache_value, fresh_value], axis=0)
    block_rows = cache_rows + count_rows
    factor = 1.0 / jnp.sqrt(jnp.float32(HD))

    def absorb(carry, key_piece, value_piece, start):
        peak, total, summed = carry
        count = key_piece.shape[0]
        tag = lax.dynamic_slice_in_dim(key_tag, start, count)
        seen = tag[None, :] <= own_order[:, None]
        score = (
            jnp.einsum(
                "qhgd,khd->hgqk",
                query,
                key_piece.reshape(count, kv_local, HD),
                preferred_element_type=jnp.float32,
            )
            * factor
        )
        score = jnp.where(seen[None, None], score, -jnp.inf)
        higher = jnp.maximum(peak, jnp.max(score, axis=-1))
        shrink = jnp.exp(peak - higher)
        weights = jnp.exp(score - higher[..., None])
        total = total * shrink + jnp.sum(weights, axis=-1)
        added = jnp.einsum(
            "hgqk,khd->hgqd",
            weights.astype(jnp.bfloat16),
            value_piece.reshape(count, kv_local, HD),
            preferred_element_type=jnp.float32,
        )
        summed = summed * shrink[..., None] + added
        return (higher, total, summed)

    initial = (
        jnp.full((kv_local, groups, count_rows), -1e30, jnp.float32),
        jnp.zeros((kv_local, groups, count_rows), jnp.float32),
        jnp.zeros((kv_local, groups, count_rows, HD), jnp.float32),
    )
    carry = initial
    key_piece = lax.all_gather(keys, "ctx", axis=0, tiled=True)
    value_piece = lax.all_gather(values, "ctx", axis=0, tiled=True)
    count = key_piece.shape[0]
    number = count // block_rows
    key_blocks = key_piece.reshape(number, block_rows, key_piece.shape[1])
    value_blocks = value_piece.reshape(number, block_rows, value_piece.shape[1])
    starts = jnp.arange(number) * block_rows

    def advance(state, item):
        return (absorb(state, item[0], item[1], item[2]), None)

    carry, unused = lax.scan(advance, carry, (key_blocks, value_blocks, starts))
    peak, total, summed = carry
    result = summed / total[..., None]
    result = jnp.transpose(result, (2, 0, 1, 3)).reshape(count_rows, kv_local * groups * HD)
    result = (result * query_live[:, None]).astype(jnp.bfloat16)
    return result


def solution(mesh):
    in_specs = (
        P("ctx", "tp"),
        P(),
        P(None, "tp"),
        P("tp"),
        P(None, "tp"),
        P("tp"),
        P(None, "tp"),
        P("tp"),
        P("ctx", "tp"),
        P("ctx", "tp"),
        P(),
        P(),
    )
    out_specs = P("ctx", "tp")
    return jax.shard_map(local, mesh=mesh, in_specs=in_specs, out_specs=out_specs, check_vma=False)
```

profile of v0, /device:TPU:0, one launch (start us, length us, event | category | flops | bytes accessed | tf_op | source)
XLA Modules:
  0.0 137.8 jit_solution(11754912918624157827)
XLA Ops:
  0.0 0.8 constant_dynamic-slice_fusion.1
  0.8 0.6 gather_fusion
  1.4 0.2 cosine_bitcast_fusion
  1.6 11.0 %all_gather.9 = bf16[128,3584]{1,0:T(8,128)(2,1)S(1)} all-gather(bf16[128,896]{1,0:T(8,128)(2,1)} %param.14), channel_id=1, replica_groups=mesh['ctx'=8,'tp'=4] {'tp'}, dimensions={1}, use_global_device_ids=true | all-gather | bytes 1146880 | tf_op jit(solution)/shard_map/all_gather | solution.py:60
  12.6 0.3 fusion.18
  12.9 0.6 convolution_add_fusion.2
  13.6 4.0 %convolution_add_fusion = f32[128,896]{1,0:T(8,128)S(1)} fusion(bf16[3584,896]{1,0:T(8,128)(2,1)} %param.16, f32[896]{0:T(1024)S(1)} %copy-done.6, bf16[128,3584]{1,0:T(8,128)(2,1)S(1)} %all_gather.9, f32[3584]{0:T(1024)S(1)} %copy-done.4, f32[128]{0:T(128)S(1)} %add_rsqrt_fusion), kind=kOutput, calls=%fused_computation.33 | convolution fusion | flops 824033280 | bytes 7817216 | tf_op jit(solution)/shard_map/dot_general | solution.py:65
  18.1 0.8 mul.122
  18.9 1.2 copy.21
  20.8 34.0 %all_gather.10 = bf16[3072,128]{1,0:T(8,128)(2,1)} all-gather(bf16[384,128]{1,0:T(8,128)(2,1)S(1)} %pad_maximum_fusion), channel_id=1, replica_groups=mesh['ctx'=8,'tp'=4] {'ctx'}, dimensions={0}, use_global_device_ids=true | all-gather | bytes 884736 | tf_op jit(solution)/shard_map/all_gather | solution.py:113
  55.1 0.3 reduce_window_sum.18
  55.5 0.5 fusion.21
  56.0 34.0 %all_gather.11 = bf16[3072,128]{1,0:T(8,128)(2,1)} all-gather(bf16[384,128]{1,0:T(8,128)(2,1)S(1)} %pad_maximum_fusion.1), channel_id=1, replica_groups=mesh['ctx'=8,'tp'=4] {'ctx'}, dimensions={0}, use_global_device_ids=true | all-gather | bytes 884736 | tf_op jit(solution)/shard_map/all_gather | solution.py:114
  90.0 46.6 %while.15 = (s32[]{:T(128)}, f32[1,7,128]{2,1,0:T(8,128)S(1)}, f32[1,7,128]{2,1,0:T(8,128)S(1)}, f32[1,7,128,128]{3,2,1,0:T(8,128)S(1)}, s32[8]{0:T(128)S(1)}, /...) while((s32[]{:T(128)}, f32[1,7,128]{2,1,0:T(8,128)S(1)}, ...), condition=%wide.region_7.8_spmd.clone, body=%wide.region_4.7_spmd.clone.sunk | while | flops 179655936 | bytes 5732539 | solution.py:124
  90.0 0.7 dynamic_slice.56
  92.8 1.3 select_reduce_fusion.2
  94.1 1.4 %fusion.45 = f32[1,7,128,128]{3,2,1,0:T(8,128)S(1)} fusion(f32[1,7,128,384]{2,3,1,0:T(8,128)S(1)} %get-tuple-element.215, f32[7,128]{1,0:T(8,128)S(1)} %bitcast.92, pred[128,384]{0,1:T(8,128)(4,1)S(1)} %broadcast_compare_fusion.2, f32[1,7,128,128]{3,2,1,0:T(8,128)S(1)} %get-tuple-element.233, f32[7,128]{1,0:T(8,128)S(1)} %get-tuple-element.216, ...), kind=kOutput, calls=%fused_computation.6.clone.1 | convolution fusion | flops 89456640 | bytes 2448897 | tf_op jit(solution)/shard_map/while/body/eval_jaxpr/hgqk,khd->hgqd/dot_general | solution.py:98
  95.6 0.3 fusion.44
  95.9 0.7 dynamic_slice.56
  98.7 1.3 select_reduce_fusion.2
  100.0 1.4 %fusion.45 = f32[1,7,128,128]{3,2,1,0:T(8,128)S(1)} fusion(f32[1,7,128,384]{2,3,1,0:T(8,128)S(1)} %get-tuple-element.215, f32[7,128]{1,0:T(8,128)S(1)} %bitcast.92, pred[128,384]{0,1:T(8,128)(4,1)S(1)} %broadcast_compare_fusion.2, f32[1,7,128,128]{3,2,1,0:T(8,128)S(1)} %get-tuple-element.233, f32[7,128]{1,0:T(8,128)S(1)} %get-tuple-element.216, ...), kind=kOutput, calls=%fused_computation.6.clone.1 | convolution fusion | flops 89456640 | bytes 2448897 | tf_op jit(solution)/shard_map/while/body/eval_jaxpr/hgqk,khd->hgqd/dot_general | solution.py:98
  101.4 0.3 fusion.44
  101.7 0.7 dynamic_slice.56
  104.5 1.3 select_reduce_fusion.2
  105.8 1.4 %fusion.45 = f32[1,7,128,128]{3,2,1,0:T(8,128)S(1)} fusion(f32[1,7,128,384]{2,3,1,0:T(8,128)S(1)} %get-tuple-element.215, f32[7,128]{1,0:T(8,128)S(1)} %bitcast.92, pred[128,384]{0,1:T(8,128)(4,1)S(1)} %broadcast_compare_fusion.2, f32[1,7,128,128]{3,2,1,0:T(8,128)S(1)} %get-tuple-element.233, f32[7,128]{1,0:T(8,128)S(1)} %get-tuple-element.216, ...), kind=kOutput, calls=%fused_computation.6.clone.1 | convolution fusion | flops 89456640 | bytes 2448897 | tf_op jit(solution)/shard_map/while/body/eval_jaxpr/hgqk,khd->hgqd/dot_general | solution.py:98
  107.2 0.3 fusion.44
  107.5 0.7 dynamic_slice.56
  110.3 1.3 select_reduce_fusion.2
  111.6 1.4 %fusion.45 = f32[1,7,128,128]{3,2,1,0:T(8,128)S(1)} fusion(f32[1,7,128,384]{2,3,1,0:T(8,128)S(1)} %get-tuple-element.215, f32[7,128]{1,0:T(8,128)S(1)} %bitcast.92, pred[128,384]{0,1:T(8,128)(4,1)S(1)} %broadcast_compare_fusion.2, f32[1,7,128,128]{3,2,1,0:T(8,128)S(1)} %get-tuple-element.233, f32[7,128]{1,0:T(8,128)S(1)} %get-tuple-element.216, ...), kind=kOutput, calls=%fused_computation.6.clone.1 | convolution fusion | flops 89456640 | bytes 2448897 | tf_op jit(solution)/shard_map/while/body/eval_jaxpr/hgqk,khd->hgqd/dot_general | solution.py:98
  113.1 0.3 fusion.44
  113.4 0.7 dynamic_slice.56
  116.1 1.3 select_reduce_fusion.2
  117.4 1.4 %fusion.45 = f32[1,7,128,128]{3,2,1,0:T(8,128)S(1)} fusion(f32[1,7,128,384]{2,3,1,0:T(8,128)S(1)} %get-tuple-element.215, f32[7,128]{1,0:T(8,128)S(1)} %bitcast.92, pred[128,384]{0,1:T(8,128)(4,1)S(1)} %broadcast_compare_fusion.2, f32[1,7,128,128]{3,2,1,0:T(8,128)S(1)} %get-tuple-element.233, f32[7,128]{1,0:T(8,128)S(1)} %get-tuple-element.216, ...), kind=kOutput, calls=%fused_computation.6.clone.1 | convolution fusion | flops 89456640 | bytes 2448897 | tf_op jit(solution)/shard_map/while/body/eval_jaxpr/hgqk,khd->hgqd/dot_general | solution.py:98
  118.9 0.3 fusion.44
  119.2 0.7 dynamic_slice.56
  122.0 1.3 select_reduce_fusion.2
  123.3 1.4 %fusion.45 = f32[1,7,128,128]{3,2,1,0:T(8,128)S(1)} fusion(f32[1,7,128,384]{2,3,1,0:T(8,128)S(1)} %get-tuple-element.215, f32[7,128]{1,0:T(8,128)S(1)} %bitcast.92, pred[128,384]{0,1:T(8,128)(4,1)S(1)} %broadcast_compare_fusion.2, f32[1,7,128,128]{3,2,1,0:T(8,128)S(1)} %get-tuple-element.233, f32[7,128]{1,0:T(8,128)S(1)} %get-tuple-element.216, ...), kind=kOutput, calls=%fused_computation.6.clone.1 | convolution fusion | flops 89456640 | bytes 2448897 | tf_op jit(solution)/shard_map/while/body/eval_jaxpr/hgqk,khd->hgqd/dot_general | solution.py:98
  124.7 0.3 fusion.44
  125.0 0.7 dynamic_slice.56
  127.8 1.3 select_reduce_fusion.2
  129.1 1.4 %fusion.45 = f32[1,7,128,128]{3,2,1,0:T(8,128)S(1)} fusion(f32[1,7,128,384]{2,3,1,0:T(8,128)S(1)} %get-tuple-element.215, f32[7,128]{1,0:T(8,128)S(1)} %bitcast.92, pred[128,384]{0,1:T(8,128)(4,1)S(1)} %broadcast_compare_fusion.2, f32[1,7,128,128]{3,2,1,0:T(8,128)S(1)} %get-tuple-element.233, f32[7,128]{1,0:T(8,128)S(1)} %get-tuple-element.216, ...), kind=kOutput, calls=%fused_computation.6.clone.1 | convolution fusion | flops 89456640 | bytes 2448897 | tf_op jit(solution)/shard_map/while/body/eval_jaxpr/hgqk,khd->hgqd/dot_general | solution.py:98
  130.5 0.3 fusion.44
  130.8 0.7 dynamic_slice.56
  133.6 1.3 select_reduce_fusion.2
  134.9 1.4 %fusion.45 = f32[1,7,128,128]{3,2,1,0:T(8,128)S(1)} fusion(f32[1,7,128,384]{2,3,1,0:T(8,128)S(1)} %get-tuple-element.215, f32[7,128]{1,0:T(8,128)S(1)} %bitcast.92, pred[128,384]{0,1:T(8,128)(4,1)S(1)} %broadcast_compare_fusion.2, f32[1,7,128,128]{3,2,1,0:T(8,128)S(1)} %get-tuple-element.233, f32[7,128]{1,0:T(8,128)S(1)} %get-tuple-element.216, ...), kind=kOutput, calls=%fused_computation.6.clone.1 | convolution fusion | flops 89456640 | bytes 2448897 | tf_op jit(solution)/shard_map/while/body/eval_jaxpr/hgqk,khd->hgqd/dot_general | solution.py:98
  136.4 0.3 fusion.44
  136.7 0.2 copy.26
  137.0 0.8 copy.27
  (90 shorter events, 3.4 us)
Async XLA Ops:
  0.0 12.9 %copy-start = (bf16[3584,128]{1,0:T(8,128)(2,1)S(1)}, bf16[3584,128]{1,0:T(8,128)(2,1)}, u32[]{:S(2)}) copy-start(bf16[3584,128]{1,0:T(8,128)(2,1)} %param.18) | copy-start | bytes 2752516
  0.0 12.9 %copy-start.4 = (f32[3584]{0:T(1024)S(1)}, f32[3584]{0:T(1024)}, u32[]{:S(2)}) copy-start(f32[3584]{0:T(1024)} %param.15) | copy-start | bytes 43012
  0.0 12.9 %copy-start.8 = (f32[128]{0:T(128)S(1)}, f32[128]{0:T(128)}, u32[]{:S(2)}) copy-start(f32[128]{0:T(128)} %param.19) | copy-start | bytes 1540
  12.6 1.0 copy-start.6
  18.9 1.9 %copy-start.1 = (bf16[256,128]{1,0:T(8,128)(2,1)S(1)}, bf16[256,128]{1,0:T(8,128)(2,1)}, u32[]{:S(2)}) copy-start(bf16[256,128]{1,0:T(8,128)(2,1)} %param.22) | copy-start | bytes 196612
  20.2 34.7 %copy-start.3 = (s32[1024]{0:T(1024)S(1)}, s32[1024]{0:T(1024)}, u32[]{:S(2)}) copy-start(s32[1024]{0:T(1024)} %param.24) | copy-start | bytes 12292
  20.2 35.3 %copy-start.9 = (f32[128]{0:T(128)S(1)}, f32[128]{0:T(128)}, u32[]{:S(2)}) copy-start(f32[128]{0:T(128)} %param.21) | copy-start | bytes 1540
  20.3 35.2 %copy-start.5 = (f32[3584]{0:T(1024)S(1)}, f32[3584]{0:T(1024)}, u32[]{:S(2)}) copy-start(f32[3584]{0:T(1024)} %param.15) | copy-start | bytes 43012
  20.3 35.2 %copy-start.7 = (bf16[3584,128]{1,0:T(8,128)(2,1)S(1)}, bf16[3584,128]{1,0:T(8,128)(2,1)}, u32[]{:S(2)}) copy-start(bf16[3584,128]{1,0:T(8,128)(2,1)} %param.20) | copy-start | bytes 2752516
  20.6 35.4 %copy-start.2 = (bf16[256,128]{1,0:T(8,128)(2,1)S(1)}, bf16[256,128]{1,0:T(8,128)(2,1)}, u32[]{:S(2)}) copy-start(bf16[256,128]{1,0:T(8,128)(2,1)} %param.23) | copy-start | bytes 196612
where the time goes:
time: 139 us; the launch traced here: 138 us
  blocking collectives  79 us (57%)
  matrix products  26.8 us (19%)
  loops' own time  15.9 us (11%)
  local copies, waits for them, and re-layouts  11.2 us (8%)
  other arithmetic  4.59 us (3%)
    all_gather x1, blocking collectives, local(): key_piece = lax.all_gather(keys, 'ctx', axis=0, tiled=True)  34 us
    all_gather x1, blocking collectives, local(): value_piece = lax.all_gather(values, 'ctx', axis=0, tiled=True)  34 us
    another operation x1, loops' own time, local(): carry, unused = lax.scan(advance, carry, (key_blocks, value_blocks, starts))  15.9 us
    dot_general x8, matrix products, absorb(): jnp.einsum('hgqk,khd->hgqd', weights.astype(jnp.bfloat16), value_piece.re...  11.5 us
    all_gather x1, blocking collectives, local(): whole = lax.all_gather(hidden, 'tp', axis=1, tiled=True)  11 us
    dot_general x8, matrix products, absorb(): jnp.einsum('qhgd,khd->hgqk', query, key_piece.reshape(count, kv_local, HD...  10.2 us
    dynamic_slice x8, local copies, waits for them, and re-layouts, local(): carry, unused = lax.scan(advance, carry, (key_blocks, value_blocks, starts))  5.24 us
    dot_general x1, matrix products, local(): jnp.dot(normed, w_query, preferred_element_type=jnp.float32) + bias_query  4.02 us

commit v1 on v0

--- a/solution.py
+++ b/solution.py
@@ -110,8 +110,11 @@
         jnp.zeros((kv_local, groups, count_rows, HD), jnp.float32),
     )
     carry = initial
-    key_piece = lax.all_gather(keys, "ctx", axis=0, tiled=True)
-    value_piece = lax.all_gather(values, "ctx", axis=0, tiled=True)
+    key_piece, value_piece = jnp.split(
+        lax.all_gather(jnp.concatenate([keys, values], axis=1), "ctx", axis=0, tiled=True),
+        [keys.shape[1]],
+        axis=1,
+    )
     count = key_piece.shape[0]
     number = count // block_rows
     key_blocks = key_piece.reshape(number, block_rows, key_piece.shape[1])

time: 139 us -> 126 us (0.906)
  blocking collectives: 79 us -> 11.2 us
  waiting for transfers between devices: 0 us -> 39.2 us
  between operations: 0.27 us -> 13.7 us
    all_gather x2 -> x0, blocking collectives: 68 us -> none  [the longest x1 34 us: local(): key_piece = lax.all_gather(keys, 'ctx', axis=0, tiled=True)]
    all_gather x0 -> x1, waiting for transfers between devices: none -> 39.2 us  [local(): lax.all_gather(jnp.concatenate([keys, values], axis=1), 'ctx', axis=0, ti...]
    split x0 -> x1, local copies, waits for them, and re-layouts: none -> 2.63 us  [local(): jnp.split(lax.all_gather(jnp.concatenate([keys, values], axis=1), 'ctx',...]
    mul x3, local copies, waits for them, and re-layouts: 2.24 us -> 0.43 us  [rotate(): return (x * cosine + turned * sine).reshape(count, heads * HD)]
  transfers between devices with their start and end apart: 0 -> 1, of which waited for: 0 -> 1; matrix products, arithmetic and copies ran while one was open for 0% -> 5% of each run, Pallas kernels for 0% -> 0%
where the time goes in v1:
time: 126 us; the launch traced here: 125 us
  waiting for transfers between devices  39.2 us (31%)
  matrix products  27.9 us (22%)
  loops' own time  16.1 us (13%)
  between operations  13.7 us (11%)
  local copies, waits for them, and re-layouts  11.5 us (9%)
  blocking collectives  11.2 us (9%)
  other arithmetic  5.23 us (4%)
    all_gather x1, waiting for transfers between devices, local(): lax.all_gather(jnp.concatenate([keys, values], axis=1), 'ctx', axis=0, ti...  39.2 us
    another operation x1, loops' own time, local(): carry, unused = lax.scan(advance, carry, (key_blocks, value_blocks, starts))  16.1 us
    dot_general x8, matrix products, absorb(): jnp.einsum('hgqk,khd->hgqd', weights.astype(jnp.bfloat16), value_piece.re...  11.5 us
    all_gather x1, blocking collectives, local(): whole = lax.all_gather(hidden, 'tp', axis=1, tiled=True)  11.2 us
    dot_general x8, matrix products, absorb(): jnp.einsum('qhgd,khd->hgqk', query, key_piece.reshape(count, kv_local, HD...  10.2 us
    dynamic_slice x8, local copies, waits for them, and re-layouts, local(): carry, unused = lax.scan(advance, carry, (key_blocks, value_blocks, starts))  4.69 us
    dot_general x1, matrix products, local(): jnp.dot(normed, w_query, preferred_element_type=jnp.float32) + bias_query  4 us
    split x1, local copies, waits for them, and re-layouts, local(): jnp.split(lax.all_gather(jnp.concatenate([keys, values], axis=1), 'ctx',...  2.63 us
  transfers between devices with their start and end apart: 1, of which 1 were waited for; matrix products, arithmetic and copies ran while one was open for 5% of the time, Pallas kernels for 0%

profile of v1, /device:TPU:0, one launch (start us, length us, event | category | flops | bytes accessed | tf_op | source)
XLA Modules:
  0.0 124.7 jit_solution(14282304787539537300)
XLA Ops:
  6.6 11.2 %all_gather.6 = bf16[128,3584]{1,0:T(8,128)(2,1)S(1)} all-gather(bf16[128,896]{1,0:T(8,128)(2,1)} %param.14), channel_id=1, replica_groups=mesh['ctx'=8,'tp'=4] {'tp'}, dimensions={1}, use_global_device_ids=true | all-gather | bytes 1146880 | tf_op jit(solution)/shard_map/all_gather | solution.py:60
  17.8 0.3 fusion.18
  18.1 0.6 convolution_add_fusion.2
  18.7 0.7 constant_dynamic-slice_fusion.1
  19.4 0.6 gather_fusion
  20.4 1.6 %fusion.21 = bf16[128,128]{1,0:T(8,128)(2,1)S(1)} fusion(bf16[3584,128]{1,0:T(8,128)(2,1)} %param.20, f32[128]{0:T(128)S(1)} %copy-done.7, bf16[128,3584]{1,0:T(8,128)(2,1)S(1)} %all_gather.6, f32[3584]{0:T(1024)S(1)} %copy-done.4, f32[128]{0:T(128)S(1)} %add_rsqrt_fusion), kind=kOutput, calls=%fused_computation.36 | convolution fusion | flops 119308288 | bytes 1883136 | tf_op jit(solution)/shard_map/dot_general | solution.py:72
  22.0 0.7 maximum_maximum_fusion
  22.8 4.0 %convolution_add_fusion = f32[128,896]{1,0:T(8,128)S(1)} fusion(bf16[3584,896]{1,0:T(8,128)(2,1)} %param.16, f32[896]{0:T(1024)S(1)} %copy-done.5, bf16[128,3584]{1,0:T(8,128)(2,1)S(1)} %all_gather.6, f32[3584]{0:T(1024)S(1)} %copy-done.4, f32[128]{0:T(128)S(1)} %add_rsqrt_fusion), kind=kOutput, calls=%fused_computation.33 | convolution fusion | flops 824033280 | bytes 7817216 | tf_op jit(solution)/shard_map/dot_general | solution.py:65
  27.1 0.2 copy.23
  27.3 0.2 copy.21
  28.3 0.3 reduce_window_sum.18
  28.7 39.2 %all-gather.2.cloned.1.call-done = bf16[3072,256]{1,0:T(8,128)(2,1)} async-done(((bf16[384,256]{1,0:T(8,128)(2,1)}), bf16[3072,256]{1,0:T(8,128)(2,1)}) %all-gather.2.cloned.1.call-update) | async-done | bytes 1572880 | tf_op jit(solution)/shard_map/all_gather | solution.py:114
  67.9 2.6 %fusion.33 = (bf16[3072,128]{1,0:T(8,128)(2,1)}, bf16[3072,128]{1,0:T(8,128)(2,1)}) fusion(bf16[3072,256]{1,0:T(8,128)(2,1)} %all-gather.2.cloned.1.call-done), kind=kLoop, calls=%fused_computation.72 | loop fusion | bytes 3145728 | tf_op jit(solution)/shard_map/split | solution.py:113
  70.5 46.2 %while.15 = (s32[]{:T(128)}, f32[1,7,128]{2,1,0:T(8,128)S(1)}, f32[1,7,128]{2,1,0:T(8,128)S(1)}, f32[1,7,128,128]{3,2,1,0:T(8,128)S(1)}, s32[8]{0:T(128)S(1)}, /...) while((s32[]{:T(128)}, f32[1,7,128]{2,1,0:T(8,128)S(1)}, ...), condition=%wide.region_7.8_spmd.clone, body=%wide.region_4.7_spmd.clone.sunk | while | flops 179655936 | bytes 5732539 | solution.py:127
  70.5 0.6 dynamic_slice.56
  73.3 1.3 %select_reduce_fusion.2 = (f32[7,128]{1,0:T(8,128)S(1)}, f32[1,7,128,384]{2,3,1,0:T(8,128)S(1)}) fusion(pred[128,384]{0,1:T(8,128)(4,1)S(1)} %broadcast_compare_fusion.2, bf16[128,1,7,128]{3,0,2,1:T(8,128)(2,1)S(1)} %get-tuple-element.255, bf16[8,384,128]{2,1,0:T(8,128)(2,1)} %get-tuple-element.254, s32[]{:T(128)} %get-tuple-element.234), kind=kOutput, calls=%fused_computation.4.clone.1 | convolution fusion | flops 89111680 | bytes 1757184 | tf_op jit(solution)/shard_map/while/body/eval_jaxpr/qhgd,khd->hgqk/dot_general | solution.py:85
  74.6 1.4 %fusion.46 = f32[1,7,128,128]{3,2,1,0:T(8,128)S(1)} fusion(f32[1,7,128,384]{2,3,1,0:T(8,128)S(1)} %get-tuple-element.219, f32[7,128]{1,0:T(8,128)S(1)} %bitcast.92, pred[128,384]{0,1:T(8,128)(4,1)S(1)} %broadcast_compare_fusion.2, f32[1,7,128,128]{3,2,1,0:T(8,128)S(1)} %get-tuple-element.237, f32[7,128]{1,0:T(8,128)S(1)} %get-tuple-element.220, ...), kind=kOutput, calls=%fused_computation.6.clone.1 | convolution fusion | flops 89456640 | bytes 2448897 | tf_op jit(solution)/shard_map/while/body/eval_jaxpr/hgqk,khd->hgqd/dot_general | solution.py:98
  76.0 0.3 fusion.45
  76.3 0.6 dynamic_slice.56
  79.0 1.3 %select_reduce_fusion.2 = (f32[7,128]{1,0:T(8,128)S(1)}, f32[1,7,128,384]{2,3,1,0:T(8,128)S(1)}) fusion(pred[128,384]{0,1:T(8,128)(4,1)S(1)} %broadcast_compare_fusion.2, bf16[128,1,7,128]{3,0,2,1:T(8,128)(2,1)S(1)} %get-tuple-element.255, bf16[8,384,128]{2,1,0:T(8,128)(2,1)} %get-tuple-element.254, s32[]{:T(128)} %get-tuple-element.234), kind=kOutput, calls=%fused_computation.4.clone.1 | convolution fusion | flops 89111680 | bytes 1757184 | tf_op jit(solution)/shard_map/while/body/eval_jaxpr/qhgd,khd->hgqk/dot_general | solution.py:85
  80.3 1.4 %fusion.46 = f32[1,7,128,128]{3,2,1,0:T(8,128)S(1)} fusion(f32[1,7,128,384]{2,3,1,0:T(8,128)S(1)} %get-tuple-element.219, f32[7,128]{1,0:T(8,128)S(1)} %bitcast.92, pred[128,384]{0,1:T(8,128)(4,1)S(1)} %broadcast_compare_fusion.2, f32[1,7,128,128]{3,2,1,0:T(8,128)S(1)} %get-tuple-element.237, f32[7,128]{1,0:T(8,128)S(1)} %get-tuple-element.220, ...), kind=kOutput, calls=%fused_computation.6.clone.1 | convolution fusion | flops 89456640 | bytes 2448897 | tf_op jit(solution)/shard_map/while/body/eval_jaxpr/hgqk,khd->hgqd/dot_general | solution.py:98
  81.8 0.3 fusion.45
  82.1 0.6 dynamic_slice.56
  84.8 1.3 %select_reduce_fusion.2 = (f32[7,128]{1,0:T(8,128)S(1)}, f32[1,7,128,384]{2,3,1,0:T(8,128)S(1)}) fusion(pred[128,384]{0,1:T(8,128)(4,1)S(1)} %broadcast_compare_fusion.2, bf16[128,1,7,128]{3,0,2,1:T(8,128)(2,1)S(1)} %get-tuple-element.255, bf16[8,384,128]{2,1,0:T(8,128)(2,1)} %get-tuple-element.254, s32[]{:T(128)} %get-tuple-element.234), kind=kOutput, calls=%fused_computation.4.clone.1 | convolution fusion | flops 89111680 | bytes 1757184 | tf_op jit(solution)/shard_map/while/body/eval_jaxpr/qhgd,khd->hgqk/dot_general | solution.py:85
  86.1 1.4 %fusion.46 = f32[1,7,128,128]{3,2,1,0:T(8,128)S(1)} fusion(f32[1,7,128,384]{2,3,1,0:T(8,128)S(1)} %get-tuple-element.219, f32[7,128]{1,0:T(8,128)S(1)} %bitcast.92, pred[128,384]{0,1:T(8,128)(4,1)S(1)} %broadcast_compare_fusion.2, f32[1,7,128,128]{3,2,1,0:T(8,128)S(1)} %get-tuple-element.237, f32[7,128]{1,0:T(8,128)S(1)} %get-tuple-element.220, ...), kind=kOutput, calls=%fused_computation.6.clone.1 | convolution fusion | flops 89456640 | bytes 2448897 | tf_op jit(solution)/shard_map/while/body/eval_jaxpr/hgqk,khd->hgqd/dot_general | solution.py:98
  87.6 0.3 fusion.45
  87.9 0.6 dynamic_slice.56
  90.6 1.3 %select_reduce_fusion.2 = (f32[7,128]{1,0:T(8,128)S(1)}, f32[1,7,128,384]{2,3,1,0:T(8,128)S(1)}) fusion(pred[128,384]{0,1:T(8,128)(4,1)S(1)} %broadcast_compare_fusion.2, bf16[128,1,7,128]{3,0,2,1:T(8,128)(2,1)S(1)} %get-tuple-element.255, bf16[8,384,128]{2,1,0:T(8,128)(2,1)} %get-tuple-element.254, s32[]{:T(128)} %get-tuple-element.234), kind=kOutput, calls=%fused_computation.4.clone.1 | convolution fusion | flops 89111680 | bytes 1757184 | tf_op jit(solution)/shard_map/while/body/eval_jaxpr/qhgd,khd->hgqk/dot_general | solution.py:85
  91.9 1.4 %fusion.46 = f32[1,7,128,128]{3,2,1,0:T(8,128)S(1)} fusion(f32[1,7,128,384]{2,3,1,0:T(8,128)S(1)} %get-tuple-element.219, f32[7,128]{1,0:T(8,128)S(1)} %bitcast.92, pred[128,384]{0,1:T(8,128)(4,1)S(1)} %broadcast_compare_fusion.2, f32[1,7,128,128]{3,2,1,0:T(8,128)S(1)} %get-tuple-element.237, f32[7,128]{1,0:T(8,128)S(1)} %get-tuple-element.220, ...), kind=kOutput, calls=%fused_computation.6.clone.1 | convolution fusion | flops 89456640 | bytes 2448897 | tf_op jit(solution)/shard_map/while/body/eval_jaxpr/hgqk,khd->hgqd/dot_general | solution.py:98
  93.3 0.3 fusion.45
  93.6 0.6 dynamic_slice.56
  96.4 1.3 %select_reduce_fusion.2 = (f32[7,128]{1,0:T(8,128)S(1)}, f32[1,7,128,384]{2,3,1,0:T(8,128)S(1)}) fusion(pred[128,384]{0,1:T(8,128)(4,1)S(1)} %broadcast_compare_fusion.2, bf16[128,1,7,128]{3,0,2,1:T(8,128)(2,1)S(1)} %get-tuple-element.255, bf16[8,384,128]{2,1,0:T(8,128)(2,1)} %get-tuple-element.254, s32[]{:T(128)} %get-tuple-element.234), kind=kOutput, calls=%fused_computation.4.clone.1 | convolution fusion | flops 89111680 | bytes 1757184 | tf_op jit(solution)/shard_map/while/body/eval_jaxpr/qhgd,khd->hgqk/dot_general | solution.py:85
  97.7 1.4 %fusion.46 = f32[1,7,128,128]{3,2,1,0:T(8,128)S(1)} fusion(f32[1,7,128,384]{2,3,1,0:T(8,128)S(1)} %get-tuple-element.219, f32[7,128]{1,0:T(8,128)S(1)} %bitcast.92, pred[128,384]{0,1:T(8,128)(4,1)S(1)} %broadcast_compare_fusion.2, f32[1,7,128,128]{3,2,1,0:T(8,128)S(1)} %get-tuple-element.237, f32[7,128]{1,0:T(8,128)S(1)} %get-tuple-element.220, ...), kind=kOutput, calls=%fused_computation.6.clone.1 | convolution fusion | flops 89456640 | bytes 2448897 | tf_op jit(solution)/shard_map/while/body/eval_jaxpr/hgqk,khd->hgqd/dot_general | solution.py:98
  99.1 0.3 fusion.45
  99.4 0.6 dynamic_slice.56
  102.2 1.3 %select_reduce_fusion.2 = (f32[7,128]{1,0:T(8,128)S(1)}, f32[1,7,128,384]{2,3,1,0:T(8,128)S(1)}) fusion(pred[128,384]{0,1:T(8,128)(4,1)S(1)} %broadcast_compare_fusion.2, bf16[128,1,7,128]{3,0,2,1:T(8,128)(2,1)S(1)} %get-tuple-element.255, bf16[8,384,128]{2,1,0:T(8,128)(2,1)} %get-tuple-element.254, s32[]{:T(128)} %get-tuple-element.234), kind=kOutput, calls=%fused_computation.4.clone.1 | convolution fusion | flops 89111680 | bytes 1757184 | tf_op jit(solution)/shard_map/while/body/eval_jaxpr/qhgd,khd->hgqk/dot_general | solution.py:85
  103.5 1.4 %fusion.46 = f32[1,7,128,128]{3,2,1,0:T(8,128)S(1)} fusion(f32[1,7,128,384]{2,3,1,0:T(8,128)S(1)} %get-tuple-element.219, f32[7,128]{1,0:T(8,128)S(1)} %bitcast.92, pred[128,384]{0,1:T(8,128)(4,1)S(1)} %broadcast_compare_fusion.2, f32[1,7,128,128]{3,2,1,0:T(8,128)S(1)} %get-tuple-element.237, f32[7,128]{1,0:T(8,128)S(1)} %get-tuple-element.220, ...), kind=kOutput, calls=%fused_computation.6.clone.1 | convolution fusion | flops 89456640 | bytes 2448897 | tf_op jit(solution)/shard_map/while/body/eval_jaxpr/hgqk,khd->hgqd/dot_general | solution.py:98
  104.9 0.3 fusion.45
  105.2 0.6 dynamic_slice.56
  107.9 1.3 %select_reduce_fusion.2 = (f32[7,128]{1,0:T(8,128)S(1)}, f32[1,7,128,384]{2,3,1,0:T(8,128)S(1)}) fusion(pred[128,384]{0,1:T(8,128)(4,1)S(1)} %broadcast_compare_fusion.2, bf16[128,1,7,128]{3,0,2,1:T(8,128)(2,1)S(1)} %get-tuple-element.255, bf16[8,384,128]{2,1,0:T(8,128)(2,1)} %get-tuple-element.254, s32[]{:T(128)} %get-tuple-element.234), kind=kOutput, calls=%fused_computation.4.clone.1 | convolution fusion | flops 89111680 | bytes 1757184 | tf_op jit(solution)/shard_map/while/body/eval_jaxpr/qhgd,khd->hgqk/dot_general | solution.py:85
  109.2 1.4 %fusion.46 = f32[1,7,128,128]{3,2,1,0:T(8,128)S(1)} fusion(f32[1,7,128,384]{2,3,1,0:T(8,128)S(1)} %get-tuple-element.219, f32[7,128]{1,0:T(8,128)S(1)} %bitcast.92, pred[128,384]{0,1:T(8,128)(4,1)S(1)} %broadcast_compare_fusion.2, f32[1,7,128,128]{3,2,1,0:T(8,128)S(1)} %get-tuple-element.237, f32[7,128]{1,0:T(8,128)S(1)} %get-tuple-element.220, ...), kind=kOutput, calls=%fused_computation.6.clone.1 | convolution fusion | flops 89456640 | bytes 2448897 | tf_op jit(solution)/shard_map/while/body/eval_jaxpr/hgqk,khd->hgqd/dot_general | solution.py:98
  110.7 0.3 fusion.45
  111.0 0.6 dynamic_slice.56
  113.7 1.3 %select_reduce_fusion.2 = (f32[7,128]{1,0:T(8,128)S(1)}, f32[1,7,128,384]{2,3,1,0:T(8,128)S(1)}) fusion(pred[128,384]{0,1:T(8,128)(4,1)S(1)} %broadcast_compare_fusion.2, bf16[128,1,7,128]{3,0,2,1:T(8,128)(2,1)S(1)} %get-tuple-element.255, bf16[8,384,128]{2,1,0:T(8,128)(2,1)} %get-tuple-element.254, s32[]{:T(128)} %get-tuple-element.234), kind=kOutput, calls=%fused_computation.4.clone.1 | convolution fusion | flops 89111680 | bytes 1757184 | tf_op jit(solution)/shard_map/while/body/eval_jaxpr/qhgd,khd->hgqk/dot_general | solution.py:85
  115.0 1.4 %fusion.46 = f32[1,7,128,128]{3,2,1,0:T(8,128)S(1)} fusion(f32[1,7,128,384]{2,3,1,0:T(8,128)S(1)} %get-tuple-element.219, f32[7,128]{1,0:T(8,128)S(1)} %bitcast.92, pred[128,384]{0,1:T(8,128)(4,1)S(1)} %broadcast_compare_fusion.2, f32[1,7,128,128]{3,2,1,0:T(8,128)S(1)} %get-tuple-element.237, f32[7,128]{1,0:T(8,128)S(1)} %get-tuple-element.220, ...), kind=kOutput, calls=%fused_computation.6.clone.1 | convolution fusion | flops 89456640 | bytes 2448897 | tf_op jit(solution)/shard_map/while/body/eval_jaxpr/hgqk,khd->hgqd/dot_general | solution.py:98
  116.5 0.3 fusion.45
  116.7 0.2 copy.26
  117.0 0.8 copy.27
  (86 shorter events, 3.4 us)
Async XLA Ops:
  6.5 11.5 %copy-start = (bf16[3584,128]{1,0:T(8,128)(2,1)S(1)}, bf16[3584,128]{1,0:T(8,128)(2,1)}, u32[]{:S(2)}) copy-start(bf16[3584,128]{1,0:T(8,128)(2,1)} %param.18) | copy-start | bytes 2752516
  6.5 11.5 %copy-start.4 = (f32[3584]{0:T(1024)S(1)}, f32[3584]{0:T(1024)}, u32[]{:S(2)}) copy-start(f32[3584]{0:T(1024)} %param.15) | copy-start | bytes 43012
  6.5 11.5 %copy-start.6 = (f32[128]{0:T(128)S(1)}, f32[128]{0:T(128)}, u32[]{:S(2)}) copy-start(f32[128]{0:T(128)} %param.19) | copy-start | bytes 1540
  6.5 61.4 %all-gather.2.cloned.1.call-start = ((), (), s32[]{:S(2)}) async-start(), calls=%async_computation | async-start | bytes 1769472 | tf_op jit(solution)/shard_map/all_gather | solution.py:114
  17.8 2.6 %copy-start.7 = (f32[128]{0:T(128)S(1)}, f32[128]{0:T(128)}, u32[]{:S(2)}) copy-start(f32[128]{0:T(128)} %param.21) | copy-start | bytes 1540
  18.7 3.4 %copy-start.1 = (bf16[256,128]{1,0:T(8,128)(2,1)S(1)}, bf16[256,128]{1,0:T(8,128)(2,1)}, u32[]{:S(2)}) copy-start(bf16[256,128]{1,0:T(8,128)(2,1)} %param.23) | copy-start | bytes 196612
  18.7 3.4 %copy-start.2 = (bf16[256,128]{1,0:T(8,128)(2,1)S(1)}, bf16[256,128]{1,0:T(8,128)(2,1)}, u32[]{:S(2)}) copy-start(bf16[256,128]{1,0:T(8,128)(2,1)} %param.22) | copy-start | bytes 196612
  20.0 2.8 %copy-start.5 = (f32[896]{0:T(1024)S(1)}, f32[896]{0:T(1024)}, u32[]{:S(2)}) copy-start(f32[896]{0:T(1024)} %param.17) | copy-start | bytes 10756
  27.3 0.7 copy-start.3
Sparse Core Ops, SparseCore 0:
  22.9 44.9 all-gather.1
